TPU v7x, 32 devices: a whole 2x2x4 slice. The times are simulated.
32 devices in a mesh: groups: 2 (over y), space: 4 (over z), chan: 4 (over x, core).
Axes of the slice: x: 2, y: 2, z: 4, core: 2. Of those that a mesh axis runs over, the one named last changes fastest.
Arguments:
- inputs: bfloat16 [2, 128, 8, 1024], P('groups', 'chan', 'space'), parts along dimension 0, may hold values from -6 to 6
- pre_act: bfloat16 [2, 128, 8, 1024], P('groups', 'chan', 'space'), parts along dimension 0, may hold values from -6 to 6
- out_grad: bfloat16 [2, 256, 4, 256], P('groups', 'chan', 'space'), parts along dimension 0, may hold values from -12 to 12
- weight_one: bfloat16 [3, 3, 3, 128, 128], P(None, None, None, 'chan'), may hold values from -0.109375 to 0.109375
- weight_two: bfloat16 [3, 3, 3, 128, 256], P(None, None, None, 'chan'), may hold values from -0.109375 to 0.109375
Outputs:
- in_grad: bfloat16 [2, 128, 8, 1024], P('groups', 'chan', 'space'), parts along dimension 0
- filter_one_grad: float32 [6, 3, 3, 128, 128], P('groups', None, None, 'chan'), parts along dimension 0
- filter_two_grad: float32 [6, 3, 3, 128, 256], P('groups', None, None, 'chan'), parts along dimension 0
There are 2 independent parts, one for each index of `groups`. A program takes and returns all parts, laid end to end along the dimension named above; an argument that names none is the same for every part. Nothing has to cross between parts.
All inputs are finite; a program needn't handle non-finite values.
Results may differ from a plain program's by a relative error of at most 0.0049.
Values may be sent and summed in bfloat16 or wider, within the bound.
A program may use at most 64 MiB of HBM per device.

v0:
```python
import functools
import math

import jax
import jax.numpy as jnp
from jax import lax
from jax.experimental import pallas as pl
from jax.experimental.pallas import tpu as pltpu
from jax.sharding import PartitionSpec as P

TAPS = 3
leak_slope = 0.3
MESH = pl.DeviceIdType.MESH
f32, bf16 = jnp.float32, jnp.bfloat16


def nt(a, b):
    return lax.dot_general(a, b, (((1,), (1,)), ((), ())), preferred_element_type=f32)


def nn(a, b):
    return jnp.dot(a, b, preferred_element_type=f32)


def lane_iota(shape):
    return lax.broadcasted_iota(jnp.int32, shape, 1)


def moved(value, row_step, col_step, side):
    length = value.shape[1]
    offset = row_step * side + col_step
    if offset % length:
        value = pltpu.roll(value, (-offset) % length, 1)
    lane = lane_iota((1, length))
    row, col = lane // side + row_step, lane % side + col_step
    if row_step or col_step:
        keep = (row >= 0) & (row < side) & (col >= 0) & (col < side)
        value = jnp.where(keep, value, 0.0)
    return value


def one_axis(shift):
    return [(0, 1), (1, 2)] if shift == 0 else [(1, 0)]


def combos():
    result = []
    for sd in range(2):
        for sh in range(2):
            for sw in range(2):
                pairs = []
                for d, kd in one_axis(sd):
                    for a, kh in one_axis(sh):
                        for b, kw in one_axis(sw):
                            pairs.append((d * 4 + a * 2 + b, (kd * TAPS + kh) * TAPS + kw))
                result.append((sd, sh, sw, pairs))
    return result


def kernel(nc, ns, side, scales, x_ref, h_ref, g_ref, w1_ref, w2_ref,
           in_ref, f1_ref, f2_ref,
           gbuf, gsh, hcls, dmat, pbuf, xs, s1, s2, r1, r2, o1, o2,
           g_sem, n_sem, p_sem, u_sem, d_sem, rs1_sem, rs2_sem, ag1_sem, ag2_sem):
    s, c = lax.axis_index("space"), lax.axis_index("chan")
    planes, ch, cells = x_ref.shape
    goc = g_ref.shape[0]
    oside = side // 2
    ocells = g_ref.shape[1]
    taps = s1.shape[0] // ns
    count = w1_ref.shape[0]

    def at_chan(t):
        return lax.rem(c + t, nc)

    def at_space(t):
        return lax.rem(s + t, ns)

    offsets = {(i % ns, j) for i in (-1, 0, 1) for j in range(nc)}
    offsets |= {(i, 0) for i in range(ns)}
    offsets = sorted(offsets - {(0, 0)})
    barrier = pltpu.get_barrier_semaphore()
    for i, j in offsets:
        pl.semaphore_signal(barrier, inc=1, device_id={"space": at_space(i), "chan": at_chan(j)}, device_id_type=MESH)
    pl.semaphore_wait(barrier, len(offsets))

    def remote(src, dst, sem, i, where):
        return pltpu.make_async_remote_copy(
            src_ref=src, dst_ref=dst, send_sem=sem.at[0, i], recv_sem=sem.at[1, i],
            device_id=where, device_id_type=MESH)

    g_rows = pl.ds(pl.multiple_of(c * goc, goc), goc)
    g_copies = [remote(g_ref, gbuf.at[0, g_rows], g_sem, t, {"chan": at_chan(t)}) for t in range(1, nc)]
    n_copies = [remote(g_ref, gbuf.at[1, g_rows], n_sem, t,
                       {"space": lax.max(s - 1, 0), "chan": at_chan(t)}) for t in range(nc)]
    for copy in g_copies:
        copy.start()

    @pl.when(s > 0)
    def _():
        for copy in n_copies:
            copy.start()

    gbuf[0, g_rows, :] = g_ref[...]

    @pl.when(s == ns - 1)
    def _():
        gbuf[1] = jnp.zeros(gbuf.shape[1:], bf16)
        pbuf[planes + 1] = jnp.zeros(pbuf.shape[1:], bf16)

    @pl.when(s == 0)
    def _():
        pbuf[0] = jnp.zeros(pbuf.shape[1:], bf16)

    size = dmat.shape[0]
    part = size // 4
    halves = cells // size
    lane = lane_iota((1, size))
    cls, inner = lane // part, lane % part
    target = (2 * (inner // oside) + cls // 2) * side + 2 * (inner % oside) + cls % 2
    dmat[...] = jnp.where(lax.broadcasted_iota(jnp.int32, (size, size), 0) == target, 1.0, 0.0).astype(bf16)
    for half in range(halves):
        block = jnp.concatenate([h_ref[d, :, half * size:(half + 1) * size] for d in range(planes)], axis=0)
        found = nn(block, dmat[...])
        for d in range(planes):
            for k in range(4):
                hcls[d * 4 + k, :, half * part:(half + 1) * part] = found[d * ch:(d + 1) * ch, k * part:(k + 1) * part]

    for copy in g_copies:
        copy.wait_recv()
    for sd in range(2):
        if sd == 1:
            @pl.when(s < ns - 1)
            def _():
                for copy in n_copies:
                    copy.wait_recv()
        field = gbuf[sd].astype(f32)
        for sh in range(2):
            for sw in range(2):
                gsh[sd * 4 + sh * 2 + sw] = moved(field, sh, sw, oside).astype(bf16)

    total = [None] * 8
    for index, (_, _, _, pairs) in enumerate(combos()):
        weights = jnp.concatenate([w2_ref[k] for _, k in pairs], axis=0)
        found = nn(weights, gsh[index])
        for place, (k, _) in enumerate(pairs):
            piece = found[place * ch:(place + 1) * ch]
            total[k] = piece if total[k] is None else total[k] + piece
    grads = [jnp.where(hcls[k] > 0, total[k], leak_slope * total[k]).astype(bf16) for k in range(8)]

    p_rows = pl.ds(pl.multiple_of(c * ch, ch), ch)
    for half in range(halves):
        block = jnp.concatenate([
            jnp.concatenate([grads[d * 4 + k][:, half * part:(half + 1) * part] for k in range(4)], axis=1)
            for d in range(planes)], axis=0)
        found = nt(block, dmat[...]).astype(bf16)
        for d in range(planes):
            pbuf[1 + d, p_rows, half * size:(half + 1) * size] = found[d * ch:(d + 1) * ch]

    mine = pbuf.at[pl.ds(1, planes), p_rows]
    p_copies = [remote(mine, mine, p_sem, t, {"chan": at_chan(t)}) for t in range(1, nc)]
    u_copies = [remote(pbuf.at[planes, p_rows], pbuf.at[0, p_rows], u_sem, t,
                       {"space": lax.min(s + 1, ns - 1), "chan": at_chan(t)}) for t in range(nc)]
    d_copies = [remote(pbuf.at[1, p_rows], pbuf.at[planes + 1, p_rows], d_sem, t,
                       {"space": lax.max(s - 1, 0), "chan": at_chan(t)}) for t in range(nc)]

    for copy in p_copies:
        copy.start()

    @pl.when(s < ns - 1)
    def _():
        for copy in u_copies:
            copy.start()

    @pl.when(s > 0)
    def _():
        for copy in d_copies:
            copy.start()

    act = [jnp.where(hcls[k] > 0, hcls[k], leak_slope * hcls[k]).astype(bf16) for k in range(8)]
    for index, (_, _, _, pairs) in enumerate(combos()):
        found = nt(jnp.concatenate([act[k] for k, _ in pairs], axis=0), gsh[index])
        for place, (_, k) in enumerate(pairs):
            s2[k] = found[place * ch:(place + 1) * ch].astype(bf16)
    for k in range(count, s2.shape[0]):
        s2[k] = jnp.zeros(s2.shape[1:], bf16)
        s1[k] = jnp.zeros(s1.shape[1:], bf16)

    def scatter(src, dst, sem):
        copies = [remote(src.at[pl.ds(at_space(t) * taps, taps)], dst.at[t], sem, t, {"space": at_space(t)})
                  for t in range(1, ns)]
        for copy in copies:
            copy.start()
        return copies

    own_taps = pl.ds(s * taps, taps)

    def reduce(src, dst, copies, out, scale, sem):
        value = src[own_taps].astype(f32)
        for t in range(1, ns):
            copies[t - 1].wait_recv()
            value = value + dst[t].astype(f32)
        out[own_taps] = (value * scale).astype(bf16)
        gathers = [remote(out.at[own_taps], out.at[own_taps], sem, t, {"space": at_space(t)}) for t in range(1, ns)]
        for copy in gathers:
            copy.start()
        return gathers

    rs2 = scatter(s2, r2, rs2_sem)

    for d in range(planes):
        field = x_ref[d].astype(f32)
        for kh in range(TAPS):
            for kw in range(TAPS):
                k = kh * TAPS + kw
                xs[d, k * ch:(k + 1) * ch, :] = moved(field, kh - 1, kw - 1, side).astype(bf16)

    for copy in p_copies:
        copy.wait_recv()

    @pl.when(s < ns - 1)
    def _():
        for copy in d_copies:
            copy.wait_recv()

    @pl.when(s > 0)
    def _():
        for copy in u_copies:
            copy.wait_recv()

    all_ch = pbuf.shape[1]
    found = None
    for d in range(planes):
        stack = pbuf[d:d + TAPS].reshape(TAPS * all_ch, cells)
        term = nt(xs[d], stack)
        found = term if found is None else found + term
    nine = TAPS * TAPS
    for kd in range(TAPS):
        column = (TAPS - 1 - kd) * all_ch
        for k in range(nine):
            s1[kd * nine + k] = found[k * ch:(k + 1) * ch, column:column + all_ch].astype(bf16)
    rs1 = scatter(s1, r1, rs1_sem)
    ag2 = reduce(s2, r2, rs2, o2, scales[1], ag2_sem)

    weights = jnp.concatenate(
        [w1_ref[kd * nine:(kd + 1) * nine].reshape(nine * ch, all_ch) for kd in reversed(range(TAPS))], axis=1)
    for d in range(planes):
        stack = pbuf[d:d + TAPS].reshape(TAPS * all_ch, cells)
        out = nn(weights, stack)
        result = None
        for kh in range(TAPS):
            rows = None
            for kw in range(TAPS):
                k = kh * TAPS + kw
                term = moved(out[k * ch:(k + 1) * ch], 0, 1 - kw, side)
                rows = term if rows is None else rows + term
            rows = moved(rows, 1 - kh, 0, side)
            result = rows if result is None else result + rows
        in_ref[d] = result.astype(bf16)

    ag1 = reduce(s1, r1, rs1, o1, scales[0], ag1_sem)
    for copy in ag2:
        copy.wait_recv()
    f2_ref[...] = o2[0:count].astype(f32)
    for copy in ag1:
        copy.wait_recv()
    f1_ref[...] = o1[0:count].astype(f32)

    for copy in g_copies + p_copies + rs1 + rs2 + ag1 + ag2:
        copy.wait_send()

    @pl.when(s > 0)
    def _():
        for copy in n_copies + d_copies:
            copy.wait_send()

    @pl.when(s < ns - 1)
    def _():
        for copy in u_copies:
            copy.wait_send()


def shards(nc, ns, inputs, pre_act, out_grad, weight_one, weight_two):
    samples, ch, planes, cells = inputs.shape
    goc, oplanes, ocells = out_grad.shape[1:]
    assert samples == 1 and planes == 2 and oplanes == 1
    side = math.isqrt(cells)
    count = TAPS ** 3
    x = jnp.swapaxes(inputs[0], 0, 1)
    h = jnp.swapaxes(pre_act[0], 0, 1)
    g = out_grad.reshape(goc, ocells)
    all_ch, all_goc = weight_one.shape[4], weight_two.shape[4]
    w1 = weight_one.reshape(count, ch, all_ch)
    w2 = weight_two.reshape(count, ch, all_goc)
    taps = -(-count // ns)
    size = min(cells, 4 * 128)
    scales = (1.0 / math.sqrt(samples * planes * ns * cells), 1.0 / math.sqrt(samples * oplanes * ns * ocells))
    vmem = pl.BlockSpec(memory_space=pltpu.VMEM)
    dma = pltpu.SemaphoreType.DMA
    out, one, two = pl.pallas_call(
        functools.partial(kernel, nc, ns, side, scales),
        out_shape=(
            jax.ShapeDtypeStruct((planes, ch, cells), bf16),
            jax.ShapeDtypeStruct((count, ch, all_ch), f32),
            jax.ShapeDtypeStruct((count, ch, all_goc), f32),
        ),
        in_specs=[vmem] * 5,
        out_specs=(vmem,) * 3,
        scratch_shapes=[
            pltpu.VMEM((2, all_goc, ocells), bf16),
            pltpu.VMEM((8, all_goc, ocells), bf16),
            pltpu.VMEM((8, ch, ocells), f32),
            pltpu.VMEM((size, size), bf16),
            pltpu.VMEM((planes + 2, all_ch, cells), bf16),
            pltpu.VMEM((planes, TAPS * TAPS * ch, cells), bf16),
            pltpu.VMEM((taps * ns, ch, all_ch), bf16),
            pltpu.VMEM((taps * ns, ch, all_goc), bf16),
            pltpu.VMEM((ns, taps, ch, all_ch), bf16),
            pltpu.VMEM((ns, taps, ch, all_goc), bf16),
            pltpu.VMEM((taps * ns, ch, all_ch), bf16),
            pltpu.VMEM((taps * ns, ch, all_goc), bf16),
            dma((2, nc)), dma((2, nc)), dma((2, nc)), dma((2, nc)), dma((2, nc)),
            dma((2, ns)), dma((2, ns)), dma((2, ns)), dma((2, ns)),
        ],
        compiler_params=pltpu.CompilerParams(
            collective_id=0, has_side_effects=True, vmem_limit_bytes=48 * 1024 * 1024),
    )(x, h, g, w1, w2)
    in_grad = jnp.swapaxes(out, 0, 1).reshape(inputs.shape)
    return (in_grad, one.reshape(TAPS, TAPS, TAPS, ch, all_ch), two.reshape(TAPS, TAPS, TAPS, ch, all_goc))


def solution(mesh):
    in_specs = (
        P("groups", "chan", "space", None),
        P("groups", "chan", "space", None),
        P("groups", "chan", "space", None),
        P(None, None, None, "chan", None),
        P(None, None, None, "chan", None),
    )
    out_specs = (
        P("groups", "chan", "space", None),
        P("groups", None, None, "chan", None),
        P("groups", None, None, "chan", None),
    )
    body = functools.partial(shards, mesh.shape["chan"], mesh.shape["space"])
    return jax.shard_map(body, mesh=mesh, in_specs=in_specs, out_specs=out_specs, check_vma=False)
```

profile of v0, /device:TPU:0, one launch (start us, length us, event | category | flops | bytes accessed | tf_op | source)
XLA Modules:
  0.0 52.7 jit_solution(2468682789463210114)
XLA Ops:
  0.6 0.0 copy-start
  0.6 0.0 copy-start.2
  0.7 1.1 %copy_bitcast_fusion = (bf16[2,32,1024]{2,1,0:T(8,128)(2,1)S(1)}, bf16[2,32,1024]{2,1,0:T(8,128)(2,1)S(1)}) fusion(bf16[1,32,2,1024]{3,2,1,0:T(2,128)(2,1)} %param.6, bf16[1,32,2,1024]{3,2,1,0:T(2,128)(2,1)} %param.5), kind=kLoop, calls=%fused_computation | loop fusion | bytes 524288 | tf_op jit(solution)/shard_map/transpose | solution.py:289
  1.7 0.0 copy-done
  1.8 0.0 copy-done.2
  1.8 0.0 copy-start.1
  1.8 0.9 %copy-done.1 = bf16[3,3,3,32,128]{4,3,2,1,0:T(8,128)(2,1)S(1)} copy-done((bf16[3,3,3,32,128]{4,3,2,1,0:T(8,128)(2,1)S(1)}, bf16[3,3,3,32,128]{4,3,2,1,0:T(8,128)(2,1)}, u32[]{:S(2)}) %copy-start.1) | copy-done | bytes 221208
  2.7 47.5 %shard_map.76 = (bf16[2,32,1024]{2,1,0:T(8,128)(2,1)S(1)}, f32[27,32,128]{2,1,0:T(8,128)S(1)}, f32[27,32,256]{2,1,0:T(8,128)S(1)}) custom-call(bf16[2,32,1024]{2,1,0:T(8,128)(2,1)S(1)} %get-tuple-element.13.x_ref, bf16[2,32,1024]{2,1,0:T(8,128)(2,1)S(1)} %get-tuple-element.12.h_ref, bf16[64,256]{1,0:T(8,128)(2,1)S(1)} %bitcast.21, ...), custom_call_target="tpu_custom_call" | custom-call | tf_op jit(solution)/shard_map/pallas_call | solution.py:299
  50.2 0.8 %copy.10 = bf16[1,32,2,1024]{3,2,1,0:T(2,128)(2,1)} copy(bf16[1,32,2,1024]{3,1,2,0:T(8,128)(2,1)S(1)} %bitcast.20) | data formatting | bytes 262144
  51.0 0.8 %copy.15 = f32[3,3,3,32,128]{4,3,2,1,0:T(8,128)} copy(f32[3,3,3,32,128]{4,3,2,1,0:T(8,128)S(1)} %bitcast.17) | data formatting | bytes 884736
  51.8 0.9 %copy.16 = f32[3,3,3,32,256]{4,3,2,1,0:T(8,128)} copy(f32[3,3,3,32,256]{4,3,2,1,0:T(8,128)S(1)} %bitcast.16) | data formatting | bytes 1769472
Async XLA Ops:
  0.6 1.1 %copy-start = (bf16[3,3,3,32,256]{4,3,2,1,0:T(8,128)(2,1)S(1)}, bf16[3,3,3,32,256]{4,3,2,1,0:T(8,128)(2,1)}, u32[]{:S(2)}) copy-start(bf16[3,3,3,32,256]{4,3,2,1,0:T(8,128)(2,1)} %param.9) | copy-start | bytes 1327108
  0.6 1.1 %copy-start.2 = (bf16[1,64,1,256]{3,1,2,0:T(8,128)(2,1)S(1)}, bf16[1,64,1,256]{3,1,2,0:T(8,128)(2,1)}, u32[]{:S(2)}) copy-start(bf16[1,64,1,256]{3,1,2,0:T(8,128)(2,1)} %param.7) | copy-start | bytes 98308
  1.8 0.9 %copy-start.1 = (bf16[3,3,3,32,128]{4,3,2,1,0:T(8,128)(2,1)S(1)}, bf16[3,3,3,32,128]{4,3,2,1,0:T(8,128)(2,1)}, u32[]{:S(2)}) copy-start(bf16[3,3,3,32,128]{4,3,2,1,0:T(8,128)(2,1)} %param.8) | copy-start | bytes 663556
where the time goes:
time: 52.9 us; the launch traced here: 52.7 us
  Pallas kernels  47.5 us (90%)
  local copies, waits for them, and re-layouts  4.52 us (9%)
  between operations  0.67 us (1%)
    pallas_call x1, Pallas kernels, shards(): pl.pallas_call(functools.partial(kernel, nc, ns, side, scales), out_shape...  47.5 us
    unnamed x9, local copies, waits for them, and re-layouts  3.45 us
    transpose x1, local copies, waits for them, and re-layouts, shards(): h = jnp.swapaxes(pre_act[0], 0, 1)  1.07 us

commit v1 on v0

--- a/solution.py
+++ b/solution.py
@@ -9,6 +9,8 @@
 from jax.sharding import PartitionSpec as P
 
 TAPS = 3
+LINE = 4
+CHUNKS = 4
 leak_slope = 0.3
 MESH = pl.DeviceIdType.MESH
 f32, bf16 = jnp.float32, jnp.bfloat16
@@ -59,15 +61,15 @@
 
 def kernel(nc, ns, side, scales, x_ref, h_ref, g_ref, w1_ref, w2_ref,
            in_ref, f1_ref, f2_ref,
-           gbuf, gsh, hcls, dmat, pbuf, xs, s1, s2, r1, r2, o1, o2,
-           g_sem, n_sem, p_sem, u_sem, d_sem, rs1_sem, rs2_sem, ag1_sem, ag2_sem):
+           gbuf, gsh, hcls, dmat, pbuf, xs, s1, s2, r1, r2, o1, o2, b1, b2,
+           g_sem, n_sem, p_sem, u_sem, d_sem, a1_sem, a2_sem, c1_sem, c2_sem, m1_sem, m2_sem):
     s, c = lax.axis_index("space"), lax.axis_index("chan")
     planes, ch, cells = x_ref.shape
     goc = g_ref.shape[0]
     oside = side // 2
     ocells = g_ref.shape[1]
-    taps = s1.shape[0] // ns
     count = w1_ref.shape[0]
+    line = ns == LINE
 
     def at_chan(t):
         return lax.rem(c + t, nc)
@@ -76,7 +78,8 @@
         return lax.rem(s + t, ns)
 
     offsets = {(i % ns, j) for i in (-1, 0, 1) for j in range(nc)}
-    offsets |= {(i, 0) for i in range(ns)}
+    if not line:
+        offsets |= {(i, 0) for i in range(ns)}
     offsets = sorted(offsets - {(0, 0)})
     barrier = pltpu.get_barrier_semaphore()
     for i, j in offsets:
@@ -147,7 +150,10 @@
             total[k] = piece if total[k] is None else total[k] + piece
     grads = [jnp.where(hcls[k] > 0, total[k], leak_slope * total[k]).astype(bf16) for k in range(8)]
 
-    p_rows = pl.ds(pl.multiple_of(c * ch, ch), ch)
+    def rows_of(index):
+        return pl.ds(pl.multiple_of(index * ch, ch), ch)
+
+    p_rows = rows_of(c)
     for half in range(halves):
         block = jnp.concatenate([
             jnp.concatenate([grads[d * 4 + k][:, half * part:(half + 1) * part] for k in range(4)], axis=1)
@@ -156,25 +162,50 @@
         for d in range(planes):
             pbuf[1 + d, p_rows, half * size:(half + 1) * size] = found[d * ch:(d + 1) * ch]
 
-    mine = pbuf.at[pl.ds(1, planes), p_rows]
-    p_copies = [remote(mine, mine, p_sem, t, {"chan": at_chan(t)}) for t in range(1, nc)]
-    u_copies = [remote(pbuf.at[planes, p_rows], pbuf.at[0, p_rows], u_sem, t,
-                       {"space": lax.min(s + 1, ns - 1), "chan": at_chan(t)}) for t in range(nc)]
-    d_copies = [remote(pbuf.at[1, p_rows], pbuf.at[planes + 1, p_rows], d_sem, t,
-                       {"space": lax.max(s - 1, 0), "chan": at_chan(t)}) for t in range(nc)]
-
-    for copy in p_copies:
-        copy.start()
-
-    @pl.when(s < ns - 1)
-    def _():
-        for copy in u_copies:
-            copy.start()
-
-    @pl.when(s > 0)
-    def _():
-        for copy in d_copies:
-            copy.start()
+    u_copy = remote(pbuf.at[planes, p_rows], pbuf.at[0, p_rows], u_sem, 0, {"space": lax.min(s + 1, ns - 1)})
+    d_copy = remote(pbuf.at[1, p_rows], pbuf.at[planes + 1, p_rows], d_sem, 0, {"space": lax.max(s - 1, 0)})
+
+    class Spread:
+        def __init__(self, where, sem):
+            def block(index):
+                return pbuf.at[where, rows_of(index)]
+
+            mine = block(c)
+            if nc == 4:
+                near, far = c + 1 - 2 * lax.rem(c, 2), lax.rem(c + 2, nc)
+                self.far = remote(mine, mine, sem, 2, {"chan": far})
+                self.near = remote(mine, mine, sem, 1, {"chan": near})
+                self.onward = remote(block(far), block(far), sem, 3, {"chan": near})
+                self.first, self.all = [self.far, self.near], [self.far, self.near, self.onward]
+            else:
+                self.onward = None
+                self.first = self.all = [remote(mine, mine, sem, t, {"chan": at_chan(t)}) for t in range(1, nc)]
+
+        def start(self):
+            for copy in self.first:
+                copy.start()
+
+        def forward(self):
+            if self.onward is not None:
+                self.far.wait_recv()
+                self.onward.start()
+
+        def wait_recv(self):
+            for copy in self.all if self.onward is None else [self.near, self.onward]:
+                copy.wait_recv()
+
+        def wait_send(self):
+            for copy in self.all:
+                copy.wait_send()
+
+    p_spread = Spread(pl.ds(1, planes), p_sem)
+    u_spread = Spread(0, u_sem)
+    d_spread = Spread(planes + 1, d_sem)
+    below, above = s > 0, s < ns - 1
+
+    pl.when(above)(u_copy.start)
+    pl.when(below)(d_copy.start)
+    p_spread.start()
 
     act = [jnp.where(hcls[k] > 0, hcls[k], leak_slope * hcls[k]).astype(bf16) for k in range(8)]
     for index, (_, _, _, pairs) in enumerate(combos()):
@@ -185,27 +216,106 @@
         s2[k] = jnp.zeros(s2.shape[1:], bf16)
         s1[k] = jnp.zeros(s1.shape[1:], bf16)
 
-    def scatter(src, dst, sem):
-        copies = [remote(src.at[pl.ds(at_space(t) * taps, taps)], dst.at[t], sem, t, {"space": at_space(t)})
-                  for t in range(1, ns)]
-        for copy in copies:
-            copy.start()
-        return copies
-
-    own_taps = pl.ds(s * taps, taps)
-
-    def reduce(src, dst, copies, out, scale, sem):
-        value = src[own_taps].astype(f32)
-        for t in range(1, ns):
-            copies[t - 1].wait_recv()
-            value = value + dst[t].astype(f32)
-        out[own_taps] = (value * scale).astype(bf16)
-        gathers = [remote(out.at[own_taps], out.at[own_taps], sem, t, {"space": at_space(t)}) for t in range(1, ns)]
-        for copy in gathers:
-            copy.start()
-        return gathers
-
-    rs2 = scatter(s2, r2, rs2_sem)
+    step = -(-count // (CHUNKS if line else ns))
+    pieces = [(i, min(step, count - i)) for i in range(0, count, step)]
+
+    class Sum:
+        def __init__(self, src, got, mid, out, scale, sems):
+            self.src, self.got, self.mid, self.out, self.scale = src, got, mid, out, scale
+            self.sems = sems
+            if line:
+                inner, end, mate = 1 + s // (ns - 1), (ns - 1) * (s // 2), ns - 1 - s
+                self.up, self.across, self.down = [], [], []
+                for k, (i, n) in enumerate(pieces):
+                    part, later = pl.ds(i, n), pl.ds(count + i, n)
+                    self.up.append(remote(src.at[part], got.at[part], sems[0], k, {"space": inner}))
+                    self.across.append(remote(mid.at[part], got.at[later], sems[1], k, {"space": mate}))
+                    self.down.append(remote(out.at[part], out.at[part], sems[2], k, {"space": end}))
+            else:
+                own = pl.ds(s * step, step)
+                self.scatters = [remote(src.at[pl.ds(at_space(t) * step, step)], got.at[pl.ds(t * step, step)],
+                                        sems[0], t, {"space": at_space(t)}) for t in range(1, ns)]
+                self.gathers = [remote(out.at[own], out.at[own], sems[2], t, {"space": at_space(t)})
+                                for t in range(1, ns)]
+
+        def first(self):
+            if line:
+                @pl.when(outer)
+                def _():
+                    for copy in self.up:
+                        copy.start()
+            else:
+                for copy in self.scatters:
+                    copy.start()
+
+        def second(self):
+            if line:
+                @pl.when(jnp.logical_not(outer))
+                def _():
+                    for (i, n), up, across in zip(pieces, self.up, self.across):
+                        up.wait_recv()
+                        value = self.src[i:i + n].astype(f32) + self.got[i:i + n].astype(f32)
+                        self.mid[i:i + n] = value.astype(bf16)
+                        across.start()
+
+        def third(self):
+            if line:
+                @pl.when(jnp.logical_not(outer))
+                def _():
+                    for (i, n), across, down in zip(pieces, self.across, self.down):
+                        across.wait_recv()
+                        value = self.mid[i:i + n].astype(f32) + self.got[count + i:count + i + n].astype(f32)
+                        self.out[i:i + n] = (value * self.scale).astype(bf16)
+                        down.start()
+            else:
+                own = pl.ds(s * step, step)
+                value = self.src[own].astype(f32)
+                for t, copy in enumerate(self.scatters, 1):
+                    copy.wait_recv()
+                    value = value + self.got[t * step:(t + 1) * step].astype(f32)
+                self.out[own] = (value * self.scale).astype(bf16)
+                for copy in self.gathers:
+                    copy.start()
+
+        def last(self):
+            if line:
+                @pl.when(outer)
+                def _():
+                    for copy in self.down:
+                        copy.wait_recv()
+            else:
+                for copy in self.gathers:
+                    copy.wait_recv()
+
+        def wait_send(self):
+            if line:
+                @pl.when(outer)
+                def _():
+                    for copy in self.up:
+                        copy.wait_send()
+
+                @pl.when(jnp.logical_not(outer))
+                def _():
+                    for copy in self.across + self.down:
+                        copy.wait_send()
+            else:
+                for copy in self.scatters + self.gathers:
+                    copy.wait_send()
+
+    outer = (s == 0) | (s == ns - 1)
+    sum2 = Sum(s2, r2, b2, o2, scales[1], (a2_sem, m2_sem, c2_sem))
+    sum1 = Sum(s1, r1, b1, o1, scales[0], (a1_sem, m1_sem, c1_sem))
+    sum2.first()
+
+    @pl.when(below)
+    def _():
+        u_copy.wait_recv()
+        u_spread.start()
+
+    @pl.when(above)
+    def _():
+        d_copy.wait_recv()
+        d_spread.start()
 
     for d in range(planes):
         field = x_ref[d].astype(f32)
@@ -214,18 +324,25 @@
                 k = kh * TAPS + kw
                 xs[d, k * ch:(k + 1) * ch, :] = moved(field, kh - 1, kw - 1, side).astype(bf16)
 
-    for copy in p_copies:
-        copy.wait_recv()
-
-    @pl.when(s < ns - 1)
-    def _():
-        for copy in d_copies:
-            copy.wait_recv()
-
-    @pl.when(s > 0)
-    def _():
-        for copy in u_copies:
-            copy.wait_recv()
+    p_spread.forward()
+
+    @pl.when(below)
+    def _():
+        u_spread.forward()
+
+    @pl.when(above)
+    def _():
+        d_spread.forward()
+
+    p_spread.wait_recv()
+
+    @pl.when(below)
+    def _():
+        u_spread.wait_recv()
+
+    @pl.when(above)
+    def _():
+        d_spread.wait_recv()
 
     all_ch = pbuf.shape[1]
     found = None
@@ -238,8 +355,8 @@
         column = (TAPS - 1 - kd) * all_ch
         for k in range(nine):
             s1[kd * nine + k] = found[k * ch:(k + 1) * ch, column:column + all_ch].astype(bf16)
-    rs1 = scatter(s1, r1, rs1_sem)
-    ag2 = reduce(s2, r2, rs2, o2, scales[1], ag2_sem)
+    sum1.first()
+    sum2.second()
 
     weights = jnp.concatenate(
         [w1_ref[kd * nine:(kd + 1) * nine].reshape(nine * ch, all_ch) for kd in reversed(range(TAPS))], axis=1)
@@ -257,26 +374,26 @@
             result = rows if result is None else result + rows
         in_ref[d] = result.astype(bf16)
 
-    ag1 = reduce(s1, r1, rs1, o1, scales[0], ag1_sem)
-    for copy in ag2:
-        copy.wait_recv()
+    sum2.third()
+    sum1.second()
+    sum1.third()
+    sum2.last()
     f2_ref[...] = o2[0:count].astype(f32)
-    for copy in ag1:
-        copy.wait_recv()
+    sum1.last()
     f1_ref[...] = o1[0:count].astype(f32)
 
-    for copy in g_copies + p_copies + rs1 + rs2 + ag1 + ag2:
-        copy.wait_send()
-
-    @pl.when(s > 0)
-    def _():
-        for copy in n_copies + d_copies:
-            copy.wait_send()
-
-    @pl.when(s < ns - 1)
-    def _():
-        for copy in u_copies:
-            copy.wait_send()
+    for item in g_copies + [p_spread, sum1, sum2]:
+        item.wait_send()
+
+    @pl.when(below)
+    def _():
+        for item in n_copies + [d_copy, u_spread]:
+            item.wait_send()
+
+    @pl.when(above)
+    def _():
+        for item in [u_copy, d_spread]:
+            item.wait_send()
 
 
 def shards(nc, ns, inputs, pre_act, out_grad, weight_one, weight_two):
@@ -291,7 +408,10 @@
     all_ch, all_goc = weight_one.shape[4], weight_two.shape[4]
     w1 = weight_one.reshape(count, ch, all_ch)
     w2 = weight_two.reshape(count, ch, all_goc)
-    taps = -(-count // ns)
+    line = ns == LINE
+    spread = count if line else -(-count // ns) * ns
+    got = 2 * count if line else spread
+    lanes = max(ns, CHUNKS)
     size = min(cells, 4 * 128)
     scales = (1.0 / math.sqrt(samples * planes * ns * cells), 1.0 / math.sqrt(samples * oplanes * ns * ocells))
     vmem = pl.BlockSpec(memory_space=pltpu.VMEM)
@@ -312,14 +432,16 @@
             pltpu.VMEM((size, size), bf16),
             pltpu.VMEM((planes + 2, all_ch, cells), bf16),
             pltpu.VMEM((planes, TAPS * TAPS * ch, cells), bf16),
-            pltpu.VMEM((taps * ns, ch, all_ch), bf16),
-            pltpu.VMEM((taps * ns, ch, all_goc), bf16),
-            pltpu.VMEM((ns, taps, ch, all_ch), bf16),
-            pltpu.VMEM((ns, taps, ch, all_goc), bf16),
-            pltpu.VMEM((taps * ns, ch, all_ch), bf16),
-            pltpu.VMEM((taps * ns, ch, all_goc), bf16),
+            pltpu.VMEM((spread, ch, all_ch), bf16),
+            pltpu.VMEM((spread, ch, all_goc), bf16),
+            pltpu.VMEM((got, ch, all_ch), bf16),
+            pltpu.VMEM((got, ch, all_goc), bf16),
+            pltpu.VMEM((spread, ch, all_ch), bf16),
+            pltpu.VMEM((spread, ch, all_goc), bf16),
+            pltpu.VMEM((spread, ch, all_ch), bf16),
+            pltpu.VMEM((spread, ch, all_goc), bf16),
             dma((2, nc)), dma((2, nc)), dma((2, nc)), dma((2, nc)), dma((2, nc)),
-            dma((2, ns)), dma((2, ns)), dma((2, ns)), dma((2, ns)),
+            dma((2, lanes)), dma((2, lanes)), dma((2, lanes)), dma((2, lanes)), dma((2, lanes)), dma((2, lanes)),
         ],
         compiler_params=pltpu.CompilerParams(
             collective_id=0, has_side_effects=True, vmem_limit_bytes=48 * 1024 * 1024),

time: 52.9 us -> 47.9 us (0.905)
  Pallas kernels: 47.5 us -> 42.6 us
    pallas_call x1, Pallas kernels: 47.5 us -> 42.6 us  [shards(): pl.pallas_call(functools.partial(kernel, nc, ns, side, scales), out_shape...]
where the time goes in v1:
time: 47.9 us; the launch traced here: 47.7 us
  Pallas kernels  42.6 us (89%)
  local copies, waits for them, and re-layouts  4.52 us (9%)
  between operations  0.67 us (1%)
    pallas_call x1, Pallas kernels, shards(): pl.pallas_call(functools.partial(kernel, nc, ns, side, scales), out_shape...  42.6 us
    unnamed x9, local copies, waits for them, and re-layouts  3.45 us
    transpose x1, local copies, waits for them, and re-layouts, shards(): h = jnp.swapaxes(pre_act[0], 0, 1)  1.07 us

profile of v1, /device:TPU:0, one launch (start us, length us, event | category | flops | bytes accessed | tf_op | source)
XLA Modules:
  0.0 47.7 jit_solution(4552803201913096653)
XLA Ops:
  0.6 0.0 copy-start
  0.6 0.0 copy-start.2
  0.7 1.1 %copy_bitcast_fusion = (bf16[2,32,1024]{2,1,0:T(8,128)(2,1)S(1)}, bf16[2,32,1024]{2,1,0:T(8,128)(2,1)S(1)}) fusion(bf16[1,32,2,1024]{3,2,1,0:T(2,128)(2,1)} %param.6, bf16[1,32,2,1024]{3,2,1,0:T(2,128)(2,1)} %param.5), kind=kLoop, calls=%fused_computation | loop fusion | bytes 524288 | tf_op jit(solution)/shard_map/transpose | solution.py:406
  1.7 0.0 copy-done
  1.8 0.0 copy-done.2
  1.8 0.0 copy-start.1
  1.8 0.9 %copy-done.1 = bf16[3,3,3,32,128]{4,3,2,1,0:T(8,128)(2,1)S(1)} copy-done((bf16[3,3,3,32,128]{4,3,2,1,0:T(8,128)(2,1)S(1)}, bf16[3,3,3,32,128]{4,3,2,1,0:T(8,128)(2,1)}, u32[]{:S(2)}) %copy-start.1) | copy-done | bytes 221208
  2.7 42.6 %shard_map.76 = (bf16[2,32,1024]{2,1,0:T(8,128)(2,1)S(1)}, f32[27,32,128]{2,1,0:T(8,128)S(1)}, f32[27,32,256]{2,1,0:T(8,128)S(1)}) custom-call(bf16[2,32,1024]{2,1,0:T(8,128)(2,1)S(1)} %get-tuple-element.13.x_ref, bf16[2,32,1024]{2,1,0:T(8,128)(2,1)S(1)} %get-tuple-element.12.h_ref, bf16[64,256]{1,0:T(8,128)(2,1)S(1)} %bitcast.21, ...), custom_call_target="tpu_custom_call" | custom-call | tf_op jit(solution)/shard_map/pallas_call | solution.py:419
  45.3 0.8 %copy.10 = bf16[1,32,2,1024]{3,2,1,0:T(2,128)(2,1)} copy(bf16[1,32,2,1024]{3,1,2,0:T(8,128)(2,1)S(1)} %bitcast.20) | data formatting | bytes 262144
  46.1 0.8 %copy.15 = f32[3,3,3,32,128]{4,3,2,1,0:T(8,128)} copy(f32[3,3,3,32,128]{4,3,2,1,0:T(8,128)S(1)} %bitcast.17) | data formatting | bytes 884736
  46.8 0.9 %copy.16 = f32[3,3,3,32,256]{4,3,2,1,0:T(8,128)} copy(f32[3,3,3,32,256]{4,3,2,1,0:T(8,128)S(1)} %bitcast.16) | data formatting | bytes 1769472
Async XLA Ops:
  0.6 1.1 %copy-start = (bf16[3,3,3,32,256]{4,3,2,1,0:T(8,128)(2,1)S(1)}, bf16[3,3,3,32,256]{4,3,2,1,0:T(8,128)(2,1)}, u32[]{:S(2)}) copy-start(bf16[3,3,3,32,256]{4,3,2,1,0:T(8,128)(2,1)} %param.9) | copy-start | bytes 1327108
  0.6 1.1 %copy-start.2 = (bf16[1,64,1,256]{3,1,2,0:T(8,128)(2,1)S(1)}, bf16[1,64,1,256]{3,1,2,0:T(8,128)(2,1)}, u32[]{:S(2)}) copy-start(bf16[1,64,1,256]{3,1,2,0:T(8,128)(2,1)} %param.7) | copy-start | bytes 98308
  1.8 0.9 %copy-start.1 = (bf16[3,3,3,32,128]{4,3,2,1,0:T(8,128)(2,1)S(1)}, bf16[3,3,3,32,128]{4,3,2,1,0:T(8,128)(2,1)}, u32[]{:S(2)}) copy-start(bf16[3,3,3,32,128]{4,3,2,1,0:T(8,128)(2,1)} %param.8) | copy-start | bytes 663556

commit v2 on v1

--- a/solution.py
+++ b/solution.py
@@ -10,7 +10,7 @@
 
 TAPS = 3
 LINE = 4
-CHUNKS = 4
+CHUNKS = 9
 leak_slope = 0.3
 MESH = pl.DeviceIdType.MESH
 f32, bf16 = jnp.float32, jnp.bfloat16
@@ -62,7 +62,8 @@
 def kernel(nc, ns, side, scales, x_ref, h_ref, g_ref, w1_ref, w2_ref,
            in_ref, f1_ref, f2_ref,
            gbuf, gsh, hcls, dmat, pbuf, xs, s1, s2, r1, r2, o1, o2, b1, b2,
-           g_sem, n_sem, p_sem, u_sem, d_sem, a1_sem, a2_sem, c1_sem, c2_sem, m1_sem, m2_sem):
+           g_sem, n_sem, p_sem, u_sem, d_sem, a1_sem, a2_sem, c1_sem, c2_sem, m1_sem, m2_sem,
+           hall, gall, gwide, awide, r_sem, l_sem, o_sem, os_sem):
     s, c = lax.axis_index("space"), lax.axis_index("chan")
     planes, ch, cells = x_ref.shape
     goc = g_ref.shape[0]
@@ -78,32 +79,13 @@
         return lax.rem(s + t, ns)
 
     offsets = {(i % ns, j) for i in (-1, 0, 1) for j in range(nc)}
-    if not line:
-        offsets |= {(i, 0) for i in range(ns)}
+    offsets |= {(i, 0) for i in range(ns)}
     offsets = sorted(offsets - {(0, 0)})
     barrier = pltpu.get_barrier_semaphore()
     for i, j in offsets:
         pl.semaphore_signal(barrier, inc=1, device_id={"space": at_space(i), "chan": at_chan(j)}, device_id_type=MESH)
-    pl.semaphore_wait(barrier, len(offsets))
-
-    def remote(src, dst, sem, i, where):
-        return pltpu.make_async_remote_copy(
-            src_ref=src, dst_ref=dst, send_sem=sem.at[0, i], recv_sem=sem.at[1, i],
-            device_id=where, device_id_type=MESH)
-
-    g_rows = pl.ds(pl.multiple_of(c * goc, goc), goc)
-    g_copies = [remote(g_ref, gbuf.at[0, g_rows], g_sem, t, {"chan": at_chan(t)}) for t in range(1, nc)]
-    n_copies = [remote(g_ref, gbuf.at[1, g_rows], n_sem, t,
-                       {"space": lax.max(s - 1, 0), "chan": at_chan(t)}) for t in range(nc)]
-    for copy in g_copies:
-        copy.start()
-
-    @pl.when(s > 0)
-    def _():
-        for copy in n_copies:
-            copy.start()
-
-    gbuf[0, g_rows, :] = g_ref[...]
+    if line:
+        hall[s] = h_ref[...]
 
     @pl.when(s == ns - 1)
     def _():
@@ -128,6 +110,104 @@
             for k in range(4):
                 hcls[d * 4 + k, :, half * part:(half + 1) * part] = found[d * ch:(d + 1) * ch, k * part:(k + 1) * part]
 
+    for d in range(planes):
+        field = x_ref[d].astype(f32)
+        for kh in range(TAPS):
+            for kw in range(TAPS):
+                k = kh * TAPS + kw
+                xs[d, k * ch:(k + 1) * ch, :] = moved(field, kh - 1, kw - 1, side).astype(bf16)
+
+    pl.semaphore_wait(barrier, len(offsets))
+
+    def remote(src, dst, sem, i, where):
+        return pltpu.make_async_remote_copy(
+            src_ref=src, dst_ref=dst, send_sem=sem.at[0, i], recv_sem=sem.at[1, i],
+            device_id=where, device_id_type=MESH)
+
+    class Spread:
+        def __init__(self, field, where, rows, sem, base=0):
+            def block(index):
+                return field.at[where, pl.ds(pl.multiple_of(index * rows, rows), rows)]
+
+            mine = block(c)
+            if nc == 4:
+                near, far = c + 1 - 2 * lax.rem(c, 2), lax.rem(c + 2, nc)
+                self.far = remote(mine, mine, sem, base + 2, {"chan": far})
+                self.near = remote(mine, mine, sem, base + 1, {"chan": near})
+                self.onward = remote(block(far), block(far), sem, base + 3, {"chan": near})
+                self.first, self.all = [self.far, self.near], [self.far, self.near, self.onward]
+            else:
+                self.onward = None
+                self.first = self.all = [remote(mine, mine, sem, base + t, {"chan": at_chan(t)}) for t in range(1, nc)]
+
+        def start(self):
+            for copy in self.first:
+                copy.start()
+
+        def forward(self):
+            if self.onward is not None:
+                self.far.wait_recv()
+                self.onward.start()
+
+        def wait_recv(self):
+            for copy in self.all if self.onward is None else [self.near, self.onward]:
+                copy.wait_recv()
+
+        def wait_send(self):
+            for copy in self.all:
+                copy.wait_send()
+
+    g_rows = pl.ds(pl.multiple_of(c * goc, goc), goc)
+    g_copies = [remote(g_ref, gbuf.at[0, g_rows], g_sem, t, {"chan": at_chan(t)}) for t in range(1, nc)]
+    n_copies = [remote(g_ref, gbuf.at[1, g_rows], n_sem, t,
+                       {"space": lax.max(s - 1, 0), "chan": at_chan(t)}) for t in range(nc)]
+    for copy in g_copies:
+        copy.start()
+
+    @pl.when(s > 0)
+    def _():
+        for copy in n_copies:
+            copy.start()
+
+    gbuf[0, g_rows, :] = g_ref[...]
+
+    if line:
+        to_next, to_last = {"space": lax.min(s + 1, ns - 1)}, {"space": lax.max(s - 1, 0)}
+        right, left = [], []
+        for j in range(ns - 1):
+            block = hall.at[lax.max(s - j, 0)]
+            right.append(remote(h_ref if j == 0 else block, block, r_sem, j, to_next))
+            block = hall.at[lax.min(s + j, ns - 1)]
+            left.append(remote(h_ref if j == 0 else block, block, l_sem, j, to_last))
+        others = [remote(g_ref, gall.at[s, g_rows], o_sem, j, {"space": at_space(ns - j)}) for j in range(1, ns)]
+
+        def has(j, other):
+            return None if j > 1 else (s == 0 if not other else s == ns - 1)
+
+        def maybe(cond, run):
+            if cond is None:
+                run()
+            else:
+                pl.when(cond)(run)
+
+        for j in range(1, ns):
+            maybe(has(j, False), others[j - 1].start)
+        pl.when(s < ns - 1)(right[0].start)
+        pl.when(s > 0)(left[0].start)
+
+        def pass_on(j):
+            @pl.when(s >= j)
+            def _():
+                right[j - 1].wait_recv()
+
+            @pl.when(s <= ns - 1 - j)
+            def _():
+                left[j - 1].wait_recv()
+
+            if j < ns - 1:
+                pl.when((s >= j) & (s < ns - 1))(right[j].start)
+                pl.when((s <= ns - 1 - j) & (s > 0))(left[j].start)
+
     for copy in g_copies:
         copy.wait_recv()
     for sd in range(2):
@@ -165,55 +245,38 @@
     u_copy = remote(pbuf.at[planes, p_rows], pbuf.at[0, p_rows], u_sem, 0, {"space": lax.min(s + 1, ns - 1)})
     d_copy = remote(pbuf.at[1, p_rows], pbuf.at[planes + 1, p_rows], d_sem, 0, {"space": lax.max(s - 1, 0)})
 
-    class Spread:
-        def __init__(self, where, sem):
-            def block(index):
-                return pbuf.at[where, rows_of(index)]
-
-            mine = block(c)
-            if nc == 4:
-                near, far = c + 1 - 2 * lax.rem(c, 2), lax.rem(c + 2, nc)
-                self.far = remote(mine, mine, sem, 2, {"chan": far})
-                self.near = remote(mine, mine, sem, 1, {"chan": near})
-                self.onward = remote(block(far), block(far), sem, 3, {"chan": near})
-                self.first, self.all = [self.far, self.near], [self.far, self.near, self.onward]
-            else:
-                self.onward = None
-                self.first = self.all = [remote(mine, mine, sem, t, {"chan": at_chan(t)}) for t in range(1, nc)]
-
-        def start(self):
-            for copy in self.first:
-                copy.start()
-
-        def forward(self):
-            if self.onward is not None:
-                self.far.wait_recv()
-                self.onward.start()
-
-        def wait_recv(self):
-            for copy in self.all if self.onward is None else [self.near, self.onward]:
-                copy.wait_recv()
-
-        def wait_send(self):
-            for copy in self.all:
-                copy.wait_send()
-
-    p_spread = Spread(pl.ds(1, planes), p_sem)
-    u_spread = Spread(0, u_sem)
-    d_spread = Spread(planes + 1, d_sem)
+    p_spread = Spread(pbuf, pl.ds(1, planes), ch, p_sem)
+    u_spread = Spread(pbuf, 0, ch, u_sem)
+    d_spread = Spread(pbuf, planes + 1, ch, d_sem)
     below, above = s > 0, s < ns - 1
 
     pl.when(above)(u_copy.start)
     pl.when(below)(d_copy.start)
     p_spread.start()
 
-    act = [jnp.where(hcls[k] > 0, hcls[k], leak_slope * hcls[k]).astype(bf16) for k in range(8)]
-    for index, (_, _, _, pairs) in enumerate(combos()):
-        found = nt(jnp.concatenate([act[k] for k, _ in pairs], axis=0), gsh[index])
-        for place, (_, k) in enumerate(pairs):
-            s2[k] = found[place * ch:(place + 1) * ch].astype(bf16)
-    for k in range(count, s2.shape[0]):
-        s2[k] = jnp.zeros(s2.shape[1:], bf16)
+    if line:
+        wide = [Spread(gall, lax.rem(s + j, ns), goc, os_sem, j * nc) for j in range(1, ns)]
+        for j in range(1, ns):
+            def relay(j=j):
+                others[j - 1].wait_recv()
+                wide[j - 1].start()
+
+            maybe(has(j, True), relay)
+        gall[s] = gbuf[0]
+
+        @pl.when(s < ns - 1)
+        def _():
+            gall[lax.min(s + 1, ns - 1)] = gbuf[1]
+
+    if not line:
+        act = [jnp.where(hcls[k] > 0, hcls[k], leak_slope * hcls[k]).astype(bf16) for k in range(8)]
+        for index, (_, _, _, pairs) in enumerate(combos()):
+            found = nt(jnp.concatenate([act[k] for k, _ in pairs], axis=0), gsh[index])
+            for place, (_, k) in enumerate(pairs):
+                s2[k] = found[place * ch:(place + 1) * ch].astype(bf16)
+    for k in range(count, s1.shape[0]):
+        if not line:
+            s2[k] = jnp.zeros(s2.shape[1:], bf16)
         s1[k] = jnp.zeros(s1.shape[1:], bf16)
 
     step = -(-count // (CHUNKS if line else ns))
@@ -303,9 +366,12 @@
                     copy.wait_send()
 
     outer = (s == 0) | (s == ns - 1)
-    sum2 = Sum(s2, r2, b2, o2, scales[1], (a2_sem, m2_sem, c2_sem))
+    sum2 = None if line else Sum(s2, r2, b2, o2, scales[1], (a2_sem, m2_sem, c2_sem))
     sum1 = Sum(s1, r1, b1, o1, scales[0], (a1_sem, m1_sem, c1_sem))
-    sum2.first()
+    if line:
+        pass_on(1)
+    else:
+        sum2.first()
 
     @pl.when(below)
     def _():
@@ -317,14 +383,11 @@
         d_copy.wait_recv()
         d_spread.start()
 
-    for d in range(planes):
-        field = x_ref[d].astype(f32)
-        for kh in range(TAPS):
-            for kw in range(TAPS):
-                k = kh * TAPS + kw
-                xs[d, k * ch:(k + 1) * ch, :] = moved(field, kh - 1, kw - 1, side).astype(bf16)
-
     p_spread.forward()
+    if line:
+        for j in range(1, ns):
+            maybe(has(j, True), wide[j - 1].forward)
+        pass_on(2)
 
     @pl.when(below)
     def _():
@@ -356,7 +419,31 @@
         for k in range(nine):
             s1[kd * nine + k] = found[k * ch:(k + 1) * ch, column:column + all_ch].astype(bf16)
     sum1.first()
-    sum2.second()
+
+    if line:
+        pass_on(ns - 1)
+        for j in range(1, ns):
+            maybe(has(j, True), wide[j - 1].wait_recv)
+        for p in range(ns):
+            field = gall[p].astype(f32)
+            for sh in range(2):
+                for sw in range(2):
+                    gwide[sh * 2 + sw, :, p * ocells:(p + 1) * ocells] = moved(field, sh, sw, oside).astype(bf16)
+            for half in range(halves):
+                block = jnp.concatenate([hall[p, d, :, half * size:(half + 1) * size] for d in range(planes)], axis=0)
+                values = nn(block, dmat[...])
+                values = jnp.where(values > 0, values, leak_slope * values).astype(bf16)
+                for d in range(planes):
+                    for k in range(4):
+                        begin = p * ocells + half * part
+                        awide[d * 4 + k, :, begin:begin + part] = values[d * ch:(d + 1) * ch, k * part:(k + 1) * part]
+        for sd, sh, sw, pairs in combos():
+            depth = (ns - sd) * ocells
+            rows = jnp.concatenate([awide[k, :, :depth] for k, _ in pairs], axis=0)
+            values = nt(rows, gwide[sh * 2 + sw, :, sd * ocells:]) * scales[1]
+            for place, (_, k) in enumerate(pairs):
+                f2_ref[k] = values[place * ch:(place + 1) * ch]
+    sum1.second()
 
     weights = jnp.concatenate(
         [w1_ref[kd * nine:(kd + 1) * nine].reshape(nine * ch, all_ch) for kd in reversed(range(TAPS))], axis=1)
@@ -374,16 +461,25 @@
             result = rows if result is None else result + rows
         in_ref[d] = result.astype(bf16)
 
-    sum2.third()
-    sum1.second()
+    if not line:
+        sum2.third()
     sum1.third()
-    sum2.last()
-    f2_ref[...] = o2[0:count].astype(f32)
+    if not line:
+        sum2.last()
+        f2_ref[...] = o2[0:count].astype(f32)
     sum1.last()
     f1_ref[...] = o1[0:count].astype(f32)
 
-    for item in g_copies + [p_spread, sum1, sum2]:
+    for item in g_copies + [p_spread, sum1] + ([] if line else [sum2]):
         item.wait_send()
+
+    if line:
+        for j in range(1, ns):
+            maybe(has(j, False), others[j - 1].wait_send)
+            maybe(has(j, True), wide[j - 1].wait_send)
+        for j in range(ns - 1):
+            pl.when((s >= j) & (s < ns - 1))(right[j].wait_send)
+            pl.when((s <= ns - 1 - j) & (s > 0))(left[j].wait_send)
 
     @pl.when(below)
     def _():
@@ -412,6 +508,8 @@
     spread = count if line else -(-count // ns) * ns
     got = 2 * count if line else spread
     lanes = max(ns, CHUNKS)
+    spread2, got2 = (1, 1) if line else (spread, got)
+    every = ns if line else 1
     size = min(cells, 4 * 128)
     scales = (1.0 / math.sqrt(samples * planes * ns * cells), 1.0 / math.sqrt(samples * oplanes * ns * ocells))
     vmem = pl.BlockSpec(memory_space=pltpu.VMEM)
@@ -433,15 +531,20 @@
             pltpu.VMEM((planes + 2, all_ch, cells), bf16),
             pltpu.VMEM((planes, TAPS * TAPS * ch, cells), bf16),
             pltpu.VMEM((spread, ch, all_ch), bf16),
-            pltpu.VMEM((spread, ch, all_goc), bf16),
+            pltpu.VMEM((spread2, ch, all_goc), bf16),
             pltpu.VMEM((got, ch, all_ch), bf16),
-            pltpu.VMEM((got, ch, all_goc), bf16),
+            pltpu.VMEM((got2, ch, all_goc), bf16),
             pltpu.VMEM((spread, ch, all_ch), bf16),
-            pltpu.VMEM((spread, ch, all_goc), bf16),
+            pltpu.VMEM((spread2, ch, all_goc), bf16),
             pltpu.VMEM((spread, ch, all_ch), bf16),
-            pltpu.VMEM((spread, ch, all_goc), bf16),
+            pltpu.VMEM((spread2, ch, all_goc), bf16),
             dma((2, nc)), dma((2, nc)), dma((2, nc)), dma((2, nc)), dma((2, nc)),
             dma((2, lanes)), dma((2, lanes)), dma((2, lanes)), dma((2, lanes)), dma((2, lanes)), dma((2, lanes)),
+            pltpu.VMEM((every, planes, ch, cells), bf16),
+            pltpu.VMEM((every, all_goc, ocells), bf16),
+            pltpu.VMEM((4, all_goc, every * ocells), bf16),
+            pltpu.VMEM((8, ch, every * ocells), bf16),
+            dma((2, every)), dma((2, every)), dma((2, every)), dma((2, every * nc)),
         ],
         compiler_params=pltpu.CompilerParams(
             collective_id=0, has_side_effects=True, vmem_limit_bytes=48 * 1024 * 1024),

time: 47.9 us -> 42.6 us (0.89)
  Pallas kernels: 42.6 us -> 37.3 us
    pallas_call x1, Pallas kernels: 42.6 us -> 37.3 us  [shards(): pl.pallas_call(functools.partial(kernel, nc, ns, side, scales), out_shape...]
where the time goes in v2:
time: 42.6 us; the launch traced here: 42.5 us
  Pallas kernels  37.3 us (88%)
  local copies, waits for them, and re-layouts  4.52 us (11%)
  between operations  0.67 us (2%)
    pallas_call x1, Pallas kernels, shards(): pl.pallas_call(functools.partial(kernel, nc, ns, side, scales), out_shape...  37.3 us
    unnamed x9, local copies, waits for them, and re-layouts  3.45 us
    transpose x1, local copies, waits for them, and re-layouts, shards(): h = jnp.swapaxes(pre_act[0], 0, 1)  1.07 us

profile of v2, /device:TPU:0, one launch (start us, length us, event | category | flops | bytes accessed | tf_op | source)
XLA Modules:
  0.0 42.5 jit_solution(7546916133887678651)
XLA Ops:
  0.6 0.0 copy-start
  0.6 0.0 copy-start.2
  0.7 1.1 %copy_bitcast_fusion = (bf16[2,32,1024]{2,1,0:T(8,128)(2,1)S(1)}, bf16[2,32,1024]{2,1,0:T(8,128)(2,1)S(1)}) fusion(bf16[1,32,2,1024]{3,2,1,0:T(2,128)(2,1)} %param.6, bf16[1,32,2,1024]{3,2,1,0:T(2,128)(2,1)} %param.5), kind=kLoop, calls=%fused_computation | loop fusion | bytes 524288 | tf_op jit(solution)/shard_map/transpose | solution.py:502
  1.7 0.0 copy-done
  1.8 0.0 copy-done.2
  1.8 0.0 copy-start.1
  1.8 0.9 %copy-done.1 = bf16[3,3,3,32,128]{4,3,2,1,0:T(8,128)(2,1)S(1)} copy-done((bf16[3,3,3,32,128]{4,3,2,1,0:T(8,128)(2,1)S(1)}, bf16[3,3,3,32,128]{4,3,2,1,0:T(8,128)(2,1)}, u32[]{:S(2)}) %copy-start.1) | copy-done | bytes 221208
  2.7 37.3 %shard_map.76 = (bf16[2,32,1024]{2,1,0:T(8,128)(2,1)S(1)}, f32[27,32,128]{2,1,0:T(8,128)S(1)}, f32[27,32,256]{2,1,0:T(8,128)S(1)}) custom-call(bf16[2,32,1024]{2,1,0:T(8,128)(2,1)S(1)} %get-tuple-element.13.x_ref, bf16[2,32,1024]{2,1,0:T(8,128)(2,1)S(1)} %get-tuple-element.12.h_ref, bf16[64,256]{1,0:T(8,128)(2,1)S(1)} %bitcast.21, ...), custom_call_target="tpu_custom_call" | custom-call | tf_op jit(solution)/shard_map/pallas_call | solution.py:517
  40.0 0.8 %copy.10 = bf16[1,32,2,1024]{3,2,1,0:T(2,128)(2,1)} copy(bf16[1,32,2,1024]{3,1,2,0:T(8,128)(2,1)S(1)} %bitcast.20) | data formatting | bytes 262144
  40.8 0.8 %copy.15 = f32[3,3,3,32,128]{4,3,2,1,0:T(8,128)} copy(f32[3,3,3,32,128]{4,3,2,1,0:T(8,128)S(1)} %bitcast.17) | data formatting | bytes 884736
  41.6 0.9 %copy.16 = f32[3,3,3,32,256]{4,3,2,1,0:T(8,128)} copy(f32[3,3,3,32,256]{4,3,2,1,0:T(8,128)S(1)} %bitcast.16) | data formatting | bytes 1769472
Async XLA Ops:
  0.6 1.1 %copy-start = (bf16[3,3,3,32,256]{4,3,2,1,0:T(8,128)(2,1)S(1)}, bf16[3,3,3,32,256]{4,3,2,1,0:T(8,128)(2,1)}, u32[]{:S(2)}) copy-start(bf16[3,3,3,32,256]{4,3,2,1,0:T(8,128)(2,1)} %param.9) | copy-start | bytes 1327108
  0.6 1.1 %copy-start.2 = (bf16[1,64,1,256]{3,1,2,0:T(8,128)(2,1)S(1)}, bf16[1,64,1,256]{3,1,2,0:T(8,128)(2,1)}, u32[]{:S(2)}) copy-start(bf16[1,64,1,256]{3,1,2,0:T(8,128)(2,1)} %param.7) | copy-start | bytes 98308
  1.8 0.9 %copy-start.1 = (bf16[3,3,3,32,128]{4,3,2,1,0:T(8,128)(2,1)S(1)}, bf16[3,3,3,32,128]{4,3,2,1,0:T(8,128)(2,1)}, u32[]{:S(2)}) copy-start(bf16[3,3,3,32,128]{4,3,2,1,0:T(8,128)(2,1)} %param.8) | copy-start | bytes 663556

commit v3 on v2

--- a/solution.py
+++ b/solution.py
@@ -11,6 +11,7 @@
 TAPS = 3
 LINE = 4
 CHUNKS = 9
+LAG = 4
 leak_slope = 0.3
 MESH = pl.DeviceIdType.MESH
 f32, bf16 = jnp.float32, jnp.bfloat16
@@ -192,8 +193,6 @@
 
         for j in range(1, ns):
             maybe(has(j, False), others[j - 1].start)
-        pl.when(s < ns - 1)(right[0].start)
-        pl.when(s > 0)(left[0].start)
 
         def pass_on(j):
             @pl.when(s >= j)
@@ -221,6 +220,10 @@
             for sw in range(2):
                 gsh[sd * 4 + sh * 2 + sw] = moved(field, sh, sw, oside).astype(bf16)
 
+    if line:
+        pl.when(s < ns - 1)(right[0].start)
+        pl.when(s > 0)(left[0].start)
+
     total = [None] * 8
     for index, (_, _, _, pairs) in enumerate(combos()):
         weights = jnp.concatenate([w2_ref[k] for _, k in pairs], axis=0)
@@ -256,12 +259,6 @@
 
     if line:
         wide = [Spread(gall, lax.rem(s + j, ns), goc, os_sem, j * nc) for j in range(1, ns)]
-        for j in range(1, ns):
-            def relay(j=j):
-                others[j - 1].wait_recv()
-                wide[j - 1].start()
-
-            maybe(has(j, True), relay)
         gall[s] = gbuf[0]
 
         @pl.when(s < ns - 1)
@@ -311,25 +308,29 @@
                 for copy in self.scatters:
                     copy.start()
 
-        def second(self):
+        def third(self):
             if line:
+                def over(k):
+                    (i, n), up, across = pieces[k], self.up[k], self.across[k]
+                    up.wait_recv()
+                    value = self.src[i:i + n].astype(f32) + self.got[i:i + n].astype(f32)
+                    self.mid[i:i + n] = value.astype(bf16)
+                    across.start()
+
+                def back(k):
+                    (i, n), across, down = pieces[k], self.across[k], self.down[k]
+                    across.wait_recv()
+                    value = self.mid[i:i + n].astype(f32) + self.got[count + i:count + i + n].astype(f32)
+                    self.out[i:i + n] = (value * self.scale).astype(bf16)
+                    down.start()
+
                 @pl.when(jnp.logical_not(outer))
                 def _():
-                    for (i, n), up, across in zip(pieces, self.up, self.across):
-                        up.wait_recv()
-                        value = self.src[i:i + n].astype(f32) + self.got[i:i + n].astype(f32)
-                        self.mid[i:i + n] = value.astype(bf16)
-                        across.start()
-
-        def third(self):
-            if line:
-                @pl.when(jnp.logical_not(outer))
-                def _():
-                    for (i, n), across, down in zip(pieces, self.across, self.down):
-                        across.wait_recv()
-                        value = self.mid[i:i + n].astype(f32) + self.got[count + i:count + i + n].astype(f32)
-                        self.out[i:i + n] = (value * self.scale).astype(bf16)
-                        down.start()
+                    for k in range(len(pieces) + LAG):
+                        if k < len(pieces):
+                            over(k)
+                        if k >= LAG:
+                            back(k - LAG)
             else:
                 own = pl.ds(s * step, step)
                 value = self.src[own].astype(f32)
@@ -368,9 +369,7 @@
     outer = (s == 0) | (s == ns - 1)
     sum2 = None if line else Sum(s2, r2, b2, o2, scales[1], (a2_sem, m2_sem, c2_sem))
     sum1 = Sum(s1, r1, b1, o1, scales[0], (a1_sem, m1_sem, c1_sem))
-    if line:
-        pass_on(1)
-    else:
+    if not line:
         sum2.first()
 
     @pl.when(below)
@@ -383,29 +382,37 @@
         d_copy.wait_recv()
         d_spread.start()
 
+    if line:
+        pass_on(1)
     p_spread.forward()
+
+    @pl.when(below)
+    def _():
+        u_spread.forward()
+
+    @pl.when(above)
+    def _():
+        d_spread.forward()
+
+    if line:
+        pass_on(2)
+    p_spread.wait_recv()
+
+    @pl.when(below)
+    def _():
+        u_spread.wait_recv()
+
+    @pl.when(above)
+    def _():
+        d_spread.wait_recv()
+
     if line:
         for j in range(1, ns):
-            maybe(has(j, True), wide[j - 1].forward)
-        pass_on(2)
-
-    @pl.when(below)
-    def _():
-        u_spread.forward()
-
-    @pl.when(above)
-    def _():
-        d_spread.forward()
-
-    p_spread.wait_recv()
-
-    @pl.when(below)
-    def _():
-        u_spread.wait_recv()
-
-    @pl.when(above)
-    def _():
-        d_spread.wait_recv()
+            def relay(j=j):
+                others[j - 1].wait_recv()
+                wide[j - 1].start()
+
+            maybe(has(j, True), relay)
 
     all_ch = pbuf.shape[1]
     found = None
@@ -419,6 +426,30 @@
         for k in range(nine):
             s1[kd * nine + k] = found[k * ch:(k + 1) * ch, column:column + all_ch].astype(bf16)
     sum1.first()
+
+
+    weights = jnp.concatenate(
+        [w1_ref[kd * nine:(kd + 1) * nine].reshape(nine * ch, all_ch) for kd in reversed(range(TAPS))], axis=1)
+    for d in range(planes):
+        stack = pbuf[d:d + TAPS].reshape(TAPS * all_ch, cells)
+        out = nn(weights, stack)
+        result = None
+        for kh in range(TAPS):
+            rows = None
+            for kw in range(TAPS):
+                k = kh * TAPS + kw
+                term = moved(out[k * ch:(k + 1) * ch], 0, 1 - kw, side)
+                rows = term if rows is None else rows + term
+            rows = moved(rows, 1 - kh, 0, side)
+            result = rows if result is None else result + rows
+        in_ref[d] = result.astype(bf16)
+
+    if line:
+        for j in range(1, ns):
+            maybe(has(j, True), wide[j - 1].forward)
+    else:
+        sum2.third()
+    sum1.third()
 
     if line:
         pass_on(ns - 1)
@@ -443,27 +474,6 @@
             values = nt(rows, gwide[sh * 2 + sw, :, sd * ocells:]) * scales[1]
             for place, (_, k) in enumerate(pairs):
                 f2_ref[k] = values[place * ch:(place + 1) * ch]
-    sum1.second()
-
-    weights = jnp.concatenate(
-        [w1_ref[kd * nine:(kd + 1) * nine].reshape(nine * ch, all_ch) for kd in reversed(range(TAPS))], axis=1)
-    for d in range(planes):
-        stack = pbuf[d:d + TAPS].reshape(TAPS * all_ch, cells)
-        out = nn(weights, stack)
-        result = None
-        for kh in range(TAPS):
-            rows = None
-            for kw in range(TAPS):
-                k = kh * TAPS + kw
-                term = moved(out[k * ch:(k + 1) * ch], 0, 1 - kw, side)
-                rows = term if rows is None else rows + term
-            rows = moved(rows, 1 - kh, 0, side)
-            result = rows if result is None else result + rows
-        in_ref[d] = result.astype(bf16)
-
-    if not line:
-        sum2.third()
-    sum1.third()
     if not line:
         sum2.last()
         f2_ref[...] = o2[0:count].astype(f32)

time: 42.6 us -> 43 us (level)
  no operation moved by 1% of the time
where the time goes in v3:
time: 43 us; the launch traced here: 42.8 us
  Pallas kernels  37.6 us (87%)
  local copies, waits for them, and re-layouts  4.52 us (11%)
  between operations  0.67 us (2%)
    pallas_call x1, Pallas kernels, shards(): pl.pallas_call(functools.partial(kernel, nc, ns, side, scales), out_shape...  37.6 us
    unnamed x9, local copies, waits for them, and re-layouts  3.45 us
    transpose x1, local copies, waits for them, and re-layouts, shards(): h = jnp.swapaxes(pre_act[0], 0, 1)  1.07 us

profile of v3, /device:TPU:0, one launch (start us, length us, event | category | flops | bytes accessed | tf_op | source)
XLA Modules:
  0.0 42.8 jit_solution(11011079151660873219)
XLA Ops:
  0.6 0.0 copy-start
  0.6 0.0 copy-start.2
  0.7 1.1 %copy_bitcast_fusion = (bf16[2,32,1024]{2,1,0:T(8,128)(2,1)S(1)}, bf16[2,32,1024]{2,1,0:T(8,128)(2,1)S(1)}) fusion(bf16[1,32,2,1024]{3,2,1,0:T(2,128)(2,1)} %param.6, bf16[1,32,2,1024]{3,2,1,0:T(2,128)(2,1)} %param.5), kind=kLoop, calls=%fused_computation | loop fusion | bytes 524288 | tf_op jit(solution)/shard_map/transpose | solution.py:512
  1.7 0.0 copy-done
  1.8 0.0 copy-done.2
  1.8 0.0 copy-start.1
  1.8 0.9 %copy-done.1 = bf16[3,3,3,32,128]{4,3,2,1,0:T(8,128)(2,1)S(1)} copy-done((bf16[3,3,3,32,128]{4,3,2,1,0:T(8,128)(2,1)S(1)}, bf16[3,3,3,32,128]{4,3,2,1,0:T(8,128)(2,1)}, u32[]{:S(2)}) %copy-start.1) | copy-done | bytes 221208
  2.7 37.6 %shard_map.76 = (bf16[2,32,1024]{2,1,0:T(8,128)(2,1)S(1)}, f32[27,32,128]{2,1,0:T(8,128)S(1)}, f32[27,32,256]{2,1,0:T(8,128)S(1)}) custom-call(bf16[2,32,1024]{2,1,0:T(8,128)(2,1)S(1)} %get-tuple-element.13.x_ref, bf16[2,32,1024]{2,1,0:T(8,128)(2,1)S(1)} %get-tuple-element.12.h_ref, bf16[64,256]{1,0:T(8,128)(2,1)S(1)} %bitcast.21, ...), custom_call_target="tpu_custom_call" | custom-call | tf_op jit(solution)/shard_map/pallas_call | solution.py:527
  40.4 0.8 %copy.10 = bf16[1,32,2,1024]{3,2,1,0:T(2,128)(2,1)} copy(bf16[1,32,2,1024]{3,1,2,0:T(8,128)(2,1)S(1)} %bitcast.20) | data formatting | bytes 262144
  41.1 0.8 %copy.15 = f32[3,3,3,32,128]{4,3,2,1,0:T(8,128)} copy(f32[3,3,3,32,128]{4,3,2,1,0:T(8,128)S(1)} %bitcast.17) | data formatting | bytes 884736
  41.9 0.9 %copy.16 = f32[3,3,3,32,256]{4,3,2,1,0:T(8,128)} copy(f32[3,3,3,32,256]{4,3,2,1,0:T(8,128)S(1)} %bitcast.16) | data formatting | bytes 1769472
Async XLA Ops:
  0.6 1.1 %copy-start = (bf16[3,3,3,32,256]{4,3,2,1,0:T(8,128)(2,1)S(1)}, bf16[3,3,3,32,256]{4,3,2,1,0:T(8,128)(2,1)}, u32[]{:S(2)}) copy-start(bf16[3,3,3,32,256]{4,3,2,1,0:T(8,128)(2,1)} %param.9) | copy-start | bytes 1327108
  0.6 1.1 %copy-start.2 = (bf16[1,64,1,256]{3,1,2,0:T(8,128)(2,1)S(1)}, bf16[1,64,1,256]{3,1,2,0:T(8,128)(2,1)}, u32[]{:S(2)}) copy-start(bf16[1,64,1,256]{3,1,2,0:T(8,128)(2,1)} %param.7) | copy-start | bytes 98308
  1.8 0.9 %copy-start.1 = (bf16[3,3,3,32,128]{4,3,2,1,0:T(8,128)(2,1)S(1)}, bf16[3,3,3,32,128]{4,3,2,1,0:T(8,128)(2,1)}, u32[]{:S(2)}) copy-start(bf16[3,3,3,32,128]{4,3,2,1,0:T(8,128)(2,1)} %param.8) | copy-start | bytes 663556

commit v4 on v3

--- a/solution.py
+++ b/solution.py
@@ -193,6 +193,8 @@
 
         for j in range(1, ns):
             maybe(has(j, False), others[j - 1].start)
+        pl.when(s < ns - 1)(right[0].start)
+        pl.when(s > 0)(left[0].start)
 
         def pass_on(j):
             @pl.when(s >= j)
@@ -220,10 +222,6 @@
             for sw in range(2):
                 gsh[sd * 4 + sh * 2 + sw] = moved(field, sh, sw, oside).astype(bf16)
 
-    if line:
-        pl.when(s < ns - 1)(right[0].start)
-        pl.when(s > 0)(left[0].start)
-
     total = [None] * 8
     for index, (_, _, _, pairs) in enumerate(combos()):
         weights = jnp.concatenate([w2_ref[k] for _, k in pairs], axis=0)
@@ -369,7 +367,9 @@
     outer = (s == 0) | (s == ns - 1)
     sum2 = None if line else Sum(s2, r2, b2, o2, scales[1], (a2_sem, m2_sem, c2_sem))
     sum1 = Sum(s1, r1, b1, o1, scales[0], (a1_sem, m1_sem, c1_sem))
-    if not line:
+    if line:
+        pass_on(1)
+    else:
         sum2.first()
 
     @pl.when(below)
@@ -382,8 +382,6 @@
         d_copy.wait_recv()
         d_spread.start()
 
-    if line:
-        pass_on(1)
     p_spread.forward()
 
     @pl.when(below)

time: 43 us -> 41 us (0.953)
  Pallas kernels: 37.6 us -> 35.7 us
    pallas_call x1, Pallas kernels: 37.6 us -> 35.7 us  [shards(): pl.pallas_call(functools.partial(kernel, nc, ns, side, scales), out_shape...]
where the time goes in v4:
time: 41 us; the launch traced here: 40.9 us
  Pallas kernels  35.7 us (87%)
  local copies, waits for them, and re-layouts  4.52 us (11%)
  between operations  0.67 us (2%)
    pallas_call x1, Pallas kernels, shards(): pl.pallas_call(functools.partial(kernel, nc, ns, side, scales), out_shape...  35.7 us
    unnamed x9, local copies, waits for them, and re-layouts  3.45 us
    transpose x1, local copies, waits for them, and re-layouts, shards(): h = jnp.swapaxes(pre_act[0], 0, 1)  1.07 us

profile of v4, /device:TPU:0, one launch (start us, length us, event | category | flops | bytes accessed | tf_op | source)
XLA Modules:
  0.0 40.9 jit_solution(16799827603369720271)
XLA Ops:
  0.6 0.0 copy-start
  0.6 0.0 copy-start.2
  0.7 1.1 %copy_bitcast_fusion = (bf16[2,32,1024]{2,1,0:T(8,128)(2,1)S(1)}, bf16[2,32,1024]{2,1,0:T(8,128)(2,1)S(1)}) fusion(bf16[1,32,2,1024]{3,2,1,0:T(2,128)(2,1)} %param.6, bf16[1,32,2,1024]{3,2,1,0:T(2,128)(2,1)} %param.5), kind=kLoop, calls=%fused_computation | loop fusion | bytes 524288 | tf_op jit(solution)/shard_map/transpose | solution.py:510
  1.7 0.0 copy-done
  1.8 0.0 copy-done.2
  1.8 0.0 copy-start.1
  1.8 0.9 %copy-done.1 = bf16[3,3,3,32,128]{4,3,2,1,0:T(8,128)(2,1)S(1)} copy-done((bf16[3,3,3,32,128]{4,3,2,1,0:T(8,128)(2,1)S(1)}, bf16[3,3,3,32,128]{4,3,2,1,0:T(8,128)(2,1)}, u32[]{:S(2)}) %copy-start.1) | copy-done | bytes 221208
  2.7 35.7 %shard_map.76 = (bf16[2,32,1024]{2,1,0:T(8,128)(2,1)S(1)}, f32[27,32,128]{2,1,0:T(8,128)S(1)}, f32[27,32,256]{2,1,0:T(8,128)S(1)}) custom-call(bf16[2,32,1024]{2,1,0:T(8,128)(2,1)S(1)} %get-tuple-element.13.x_ref, bf16[2,32,1024]{2,1,0:T(8,128)(2,1)S(1)} %get-tuple-element.12.h_ref, bf16[64,256]{1,0:T(8,128)(2,1)S(1)} %bitcast.21, ...), custom_call_target="tpu_custom_call" | custom-call | tf_op jit(solution)/shard_map/pallas_call | solution.py:525
  38.4 0.8 %copy.10 = bf16[1,32,2,1024]{3,2,1,0:T(2,128)(2,1)} copy(bf16[1,32,2,1024]{3,1,2,0:T(8,128)(2,1)S(1)} %bitcast.20) | data formatting | bytes 262144
  39.2 0.8 %copy.15 = f32[3,3,3,32,128]{4,3,2,1,0:T(8,128)} copy(f32[3,3,3,32,128]{4,3,2,1,0:T(8,128)S(1)} %bitcast.17) | data formatting | bytes 884736
  40.0 0.9 %copy.16 = f32[3,3,3,32,256]{4,3,2,1,0:T(8,128)} copy(f32[3,3,3,32,256]{4,3,2,1,0:T(8,128)S(1)} %bitcast.16) | data formatting | bytes 1769472
Async XLA Ops:
  0.6 1.1 %copy-start = (bf16[3,3,3,32,256]{4,3,2,1,0:T(8,128)(2,1)S(1)}, bf16[3,3,3,32,256]{4,3,2,1,0:T(8,128)(2,1)}, u32[]{:S(2)}) copy-start(bf16[3,3,3,32,256]{4,3,2,1,0:T(8,128)(2,1)} %param.9) | copy-start | bytes 1327108
  0.6 1.1 %copy-start.2 = (bf16[1,64,1,256]{3,1,2,0:T(8,128)(2,1)S(1)}, bf16[1,64,1,256]{3,1,2,0:T(8,128)(2,1)}, u32[]{:S(2)}) copy-start(bf16[1,64,1,256]{3,1,2,0:T(8,128)(2,1)} %param.7) | copy-start | bytes 98308
  1.8 0.9 %copy-start.1 = (bf16[3,3,3,32,128]{4,3,2,1,0:T(8,128)(2,1)S(1)}, bf16[3,3,3,32,128]{4,3,2,1,0:T(8,128)(2,1)}, u32[]{:S(2)}) copy-start(bf16[3,3,3,32,128]{4,3,2,1,0:T(8,128)(2,1)} %param.8) | copy-start | bytes 663556
